TPU v7x, 32 devices: a whole 2x2x4 slice. The times are simulated.
32 devices in a mesh: pair: 2 (over x), seq: 4 (over z), head: 4 (over y, core).
Axes of the slice: x: 2, y: 2, z: 4, core: 2. Of those that a mesh axis runs over, the one named last changes fastest.
Arguments:
- resp_query: bfloat16 [2, 4, 256, 4096], P('pair', 'seq', None, 'head'), may hold values from -6 to 6
- resp_key: bfloat16 [2, 4, 256, 1024], P('pair', 'seq', None, 'head'), may hold values from -6 to 6
- resp_value: bfloat16 [2, 4, 256, 1024], P('pair', 'seq', None, 'head'), may hold values from -6 to 6
- direction: bfloat16 [2, 4, 256, 4096], P('pair', 'seq', None, 'head'), may hold values from -96 to 96
- ratio: float32 [2, 4, 256], P('pair', 'seq'), may hold values from -4.2 to 4.2
- lengths: int32 [2, 4], P('pair', 'seq'), may hold values from 1 to 256, 640 in all within a row
- partner: int32 [4], replicated, may hold values from 0 to 3, each once
- prompt_key: bfloat16 [1024, 1024], P('pair', 'head'), may hold values from -6 to 6
- prompt_value: bfloat16 [1024, 1024], P('pair', 'head'), may hold values from -6 to 6
Outputs:
- query_grad: bfloat16 [2, 4, 256, 4096], P('pair', 'seq', None, 'head')
- resp_key_grad: bfloat16 [2, 4, 256, 1024], P('pair', 'seq', None, 'head')
- resp_value_grad: bfloat16 [2, 4, 256, 1024], P('pair', 'seq', None, 'head')
- prompt_key_grad: bfloat16 [1024, 1024], P('pair', 'head')
- prompt_value_grad: bfloat16 [1024, 1024], P('pair', 'head')
Inputs may be any that keep to these rules, and one draw needn't show every extreme that they name: On each side the response lengths sum to 640, and the longest is 256. partner names each rejected response exactly once.
All inputs are finite; a program needn't handle non-finite values. No bound on the sum of `lengths` on one device may be relied on, other than what follows from the above.
Results may differ from a plain program's by a relative error of at most 0.03.
Values may be sent and summed in bfloat16 or wider, within the bound.
A program may use at most 64 MiB of HBM per device.

v0:
```python
import functools
import math

import jax
import jax.numpy as jnp
from jax import lax
from jax.experimental import pallas as pl
from jax.experimental.pallas import tpu as pltpu
from jax.sharding import PartitionSpec as P

HEAD_DIM = 128
DPO_BETA = 0.1
BLOCK = 256
UNIT = 128
MESH = pl.DeviceIdType.MESH
NT = (((1,), (1,)), ((), ()))
TN = (((0,), (0,)), ((), ()))
F32 = jnp.float32
BF16 = jnp.bfloat16


def dot_nt(a, b):
    return lax.dot_general(a, b, NT, preferred_element_type=F32)


def dot_tn(a, b):
    return lax.dot_general(a, b, TN, preferred_element_type=F32)


def kernel(
    n, lengths, partner, ratio, q_in, rk_in, rv_in, dir_in, pk_in, pv_in,
    qg_out, rkg_out, rvg_out, pkg_out, pvg_out,
    table, q_rows, g_rows, pk_far, pv_far, s_buf, dp_buf, ds_buf,
    x_send, x_recv, own_acc, c_send, c_recv,
    tab_send_sem, tab_recv_sem, kv_send_sem, kv_recv_sem,
    x_send_sem, x_recv_sem, c_send_sem, c_recv_sem,
):
    rows = q_in.shape[2]
    half = pk_in.shape[0]
    kv_local = rk_in.shape[3] // HEAD_DIM
    group = q_in.shape[3] // rk_in.shape[3]
    lanes = rows * group
    block = min(BLOCK, half)
    blocks = half // block
    unit = min(UNIT, block)
    units = half // unit
    scale = 1.0 / math.sqrt(HEAD_DIM)
    exp_scale = scale * math.log2(math.e)
    side = lax.axis_index("pair")
    seq = lax.axis_index("seq")
    head = lax.axis_index("head")
    flat = side * n + seq
    pair_dev = (1 - side, seq, head)

    def peer(offset):
        other = lax.rem(flat + offset, 2 * n)
        return (other // n, lax.rem(other, n), head)

    def seq_peer(offset):
        return lax.rem(seq + offset, n)

    barrier = pltpu.get_barrier_semaphore()
    for d in range(1, 2 * n):
        pl.semaphore_signal(barrier, inc=1, device_id=peer(d), device_id_type=MESH)

    kv_copies = []
    for i in range(kv_local):
        cols = pl.ds(i * HEAD_DIM, HEAD_DIM)
        for which, (src, dst) in enumerate(((pk_in, pk_far), (pv_in, pv_far))):
            slot = 2 * i + which
            copy = pltpu.make_async_remote_copy(
                src_ref=src.at[:, cols], dst_ref=dst.at[i],
                send_sem=kv_send_sem.at[slot], recv_sem=kv_recv_sem.at[slot],
                device_id=pair_dev, device_id_type=MESH,
            )
            kv_copies.append(copy)

    length = lengths[0, 0]
    position = lax.broadcasted_iota(jnp.int32, (1, rows), 1)
    own_sum = jnp.sum(jnp.where(position < length, ratio[0], 0.0), axis=1, keepdims=True)
    table[flat] = jnp.broadcast_to(own_sum, (1, HEAD_DIM))
    tab_copies = []

    def build_grads():
        for copy in tab_copies:
            copy.wait_recv()
        zero = jnp.zeros((1, HEAD_DIM), F32)
        mine = partner[seq]
        chosen, rejected = table[seq], zero
        chosen_r, rejected_r = zero, table[n + seq]
        for r in range(n):
            rejected = rejected + jnp.where(mine == r, table[n + r], 0.0)
            chosen_r = chosen_r + jnp.where(partner[r] == seq, table[r], 0.0)
        gap = jnp.where(side == 0, chosen - rejected, chosen_r - rejected_r)
        pulled = 1.0 / (1.0 + jnp.exp(DPO_BETA * gap))
        weight = jnp.where(side == 0, -pulled, pulled)
        live = lax.broadcasted_iota(jnp.int32, (rows, HEAD_DIM), 0) < length
        for i in range(kv_local):
            for g in range(group):
                cols = slice((i * group + g) * HEAD_DIM, (i * group + g + 1) * HEAD_DIM)
                value = weight * dir_in[0, 0, :, cols].astype(F32)
                g_rows[i, g * rows:(g + 1) * rows, :] = jnp.where(live, value, 0.0).astype(BF16)

    far_at, own_at, resp_at = 0, half, 2 * half

    def segments(i):
        cols = slice(i * HEAD_DIM, (i + 1) * HEAD_DIM)
        own = [
            (own_at + b * block, lambda b=b: pk_in[b * block:(b + 1) * block, cols],
             lambda b=b: pv_in[b * block:(b + 1) * block, cols])
            for b in range(blocks)
        ]
        resp = [(resp_at, lambda: rk_in[0, 0, :, cols], lambda: rv_in[0, 0, :, cols])]
        far = [
            (far_at + b * block, lambda b=b: pk_far[i, b * block:(b + 1) * block, :],
             lambda b=b: pv_far[i, b * block:(b + 1) * block, :])
            for b in range(blocks)
        ]
        return own, resp, far

    def score_block(i, at, keys, top, masked):
        scores = dot_nt(keys, q_rows[i])
        if masked:
            key_pos = lax.broadcasted_iota(jnp.int32, scores.shape, 0)
            row_pos = lax.rem(lax.broadcasted_iota(jnp.int32, scores.shape, 1), rows)
            scores = jnp.where((key_pos <= row_pos) & (key_pos < length), scores, -jnp.inf)
        s_buf[i, at:at + scores.shape[0], :] = scores
        return jnp.maximum(top, jnp.max(scores, axis=0, keepdims=True))

    def near_scores(i):
        own, resp, _ = segments(i)
        top = jnp.full((1, lanes), -jnp.inf, F32)
        for at, key, _v in own:
            top = score_block(i, at, key(), top, False)
        for at, key, _v in resp:
            top = score_block(i, at, key(), top, True)
        return top

    def far_scores(i, top):
        kv_copies[2 * i].wait_recv()
        for at, key, _v in segments(i)[2]:
            top = score_block(i, at, key(), top, False)
        return top

    def prob_grad_block(i, at, v):
        dp_buf[i, at:at + v.shape[0], :] = dot_nt(v, g_rows[i])

    def near_prob_grads(i):
        own, resp, _ = segments(i)
        for at, _k, value in own + resp:
            prob_grad_block(i, at, value())

    def exp_pass(i, top):
        own, resp, far = segments(i)
        shift = top * exp_scale
        total = jnp.zeros((1, lanes), F32)
        delta = jnp.zeros((1, lanes), F32)
        for at, _k, value in own + resp + far:
            if at == far_at:
                kv_copies[2 * i + 1].wait_recv()
            span = slice(at, at + (rows if at == resp_at else block))
            if at < own_at:
                prob_grad_block(i, at, value())
            e = jnp.exp2(s_buf[i, span, :] * exp_scale - shift)
            s_buf[i, span, :] = e
            total = total + jnp.sum(e, axis=0, keepdims=True)
            delta = delta + jnp.sum(e * dp_buf[i, span, :], axis=0, keepdims=True)
        inv = 1.0 / total
        return inv, delta * inv

    def grad_block(i, at, size, inv, delta):
        span = slice(at, at + size)
        prob = s_buf[i, span, :] * inv
        ds = (prob * (dp_buf[i, span, :] - delta)).astype(BF16)
        ds_buf[i, span, :] = ds
        dk = jnp.dot(ds, q_rows[i], preferred_element_type=F32) * scale
        dv = jnp.dot(prob.astype(BF16), g_rows[i], preferred_element_type=F32)
        return dk, dv

    def x_copy(u):
        return pltpu.make_async_remote_copy(
            src_ref=x_send.at[u], dst_ref=x_recv.at[u],
            send_sem=x_send_sem.at[u], recv_sem=x_recv_sem.at[u],
            device_id=pair_dev, device_id_type=MESH,
        )

    def far_pass(i, inv, delta):
        for b in range(blocks):
            dk, dv = grad_block(i, far_at + b * block, block, inv, delta)
            for k in range(block // unit):
                u = i * units + b * (block // unit) + k
                x_send[u, :, :HEAD_DIM] = dk[k * unit:(k + 1) * unit].astype(BF16)
                x_send[u, :, HEAD_DIM:] = dv[k * unit:(k + 1) * unit].astype(BF16)
                x_copy(u).start()

    def own_pass(i, inv, delta):
        for b in range(blocks):
            dk, dv = grad_block(i, own_at + b * block, block, inv, delta)
            own_acc[i, b * block:(b + 1) * block, :HEAD_DIM] = dk
            own_acc[i, b * block:(b + 1) * block, HEAD_DIM:] = dv

    def resp_pass(i, inv, delta):
        dk, dv = grad_block(i, resp_at, rows, inv, delta)
        cols = slice(i * HEAD_DIM, (i + 1) * HEAD_DIM)
        rkg_out[0, 0, :, cols] = dk.astype(BF16)
        rvg_out[0, 0, :, cols] = dv.astype(BF16)

    def chain_copy(u, way):
        turn = (1 - way) // 2
        return pltpu.make_async_remote_copy(
            src_ref=c_send.at[2 * u + turn], dst_ref=c_recv.at[2 * u + turn],
            send_sem=c_send_sem.at[2 * u + turn], recv_sem=c_recv_sem.at[2 * u + turn],
            device_id=(side, lax.rem(seq + way + n, n), head), device_id_type=MESH,
        )

    first_way = jnp.where(2 * seq < n, 1, -1)

    def chain_step(u, i, at, way):
        has_from = (seq - way >= 0) & (seq - way < n)
        has_to = (seq + way >= 0) & (seq + way < n)
        turn = (1 - way) // 2

        @pl.when(has_from)
        def _():
            chain_copy(u, way).wait_recv()

        @pl.when(has_to & has_from)
        def _():
            passed = own_acc[i, at:at + unit, :] + c_recv[2 * u + turn].astype(F32)
            c_send[2 * u + turn] = passed.astype(BF16)

        @pl.when(has_to & jnp.logical_not(has_from))
        def _():
            c_send[2 * u + turn] = own_acc[i, at:at + unit, :].astype(BF16)

        @pl.when(has_to)
        def _():
            chain_copy(u, way).start()

    def chain(u):
        i, at = u // units, u % units * unit
        x_copy(u).wait_recv()
        own_acc[i, at:at + unit, :] += x_recv[u].astype(F32)
        chain_step(u, i, at, first_way)

    def chain_back(u):
        i, at = u // units, u % units * unit
        chain_step(u, i, at, -first_way)
        cols = slice(i * HEAD_DIM, (i + 1) * HEAD_DIM)

        for way in (1, -1):
            @pl.when((seq - way >= 0) & (seq - way < n))
            def _():
                own_acc[i, at:at + unit, :] += c_recv[2 * u + (1 - way) // 2].astype(F32)
        pkg_out[at:at + unit, cols] = own_acc[i, at:at + unit, :HEAD_DIM].astype(BF16)
        pvg_out[at:at + unit, cols] = own_acc[i, at:at + unit, HEAD_DIM:].astype(BF16)

    def query_pass(i):
        own, resp, far = segments(i)
        total = jnp.zeros((HEAD_DIM, lanes), F32)
        for at, key, _v in own + resp + far:
            keys = key()
            total = total + dot_tn(keys, ds_buf[i, at:at + keys.shape[0], :])
        total = total * scale
        for g in range(group):
            cols = slice((i * group + g) * HEAD_DIM, (i * group + g + 1) * HEAD_DIM)
            qg_out[0, 0, :, cols] = total[:, g * rows:(g + 1) * rows].T.astype(BF16)

    count = kv_local * units
    for i in range(kv_local):
        for g in range(group):
            cols = slice((i * group + g) * HEAD_DIM, (i * group + g + 1) * HEAD_DIM)
            q_rows[i, g * rows:(g + 1) * rows, :] = q_in[0, 0, :, cols]
    tops = [near_scores(0)]
    pl.semaphore_wait(barrier, 2 * n - 1)
    for d in range(1, 2 * n):
        copy = pltpu.make_async_remote_copy(
            src_ref=table.at[flat], dst_ref=table.at[flat],
            send_sem=tab_send_sem.at[d - 1], recv_sem=tab_recv_sem.at[d - 1],
            device_id=peer(d), device_id_type=MESH,
        )
        copy.start()
        tab_copies.append(copy)
    for copy in kv_copies:
        copy.start()
    tops += [near_scores(i) for i in range(1, kv_local)]
    build_grads()
    for i in range(kv_local):
        near_prob_grads(i)
    stats = []
    for i in range(kv_local):
        stats.append(exp_pass(i, far_scores(i, tops[i])))
        far_pass(i, *stats[i])
        own_pass(i, *stats[i])
        if i > 0:
            for u in range((i - 1) * units, i * units):
                chain(u)
    for i in range(kv_local):
        resp_pass(i, *stats[i])
        query_pass(i)
    for u in range((kv_local - 1) * units, count):
        chain(u)
    for u in range(count):
        chain_back(u)
    for copy in tab_copies + kv_copies:
        copy.wait_send()
    for u in range(count):
        x_copy(u).wait_send()
        for way in (1, -1):
            @pl.when((seq + way >= 0) & (seq + way < n))
            def _():
                chain_copy(u, way).wait_send()


def store_kernel(count, *refs):
    sources, targets, held = refs[:count], refs[count:2 * count], refs[2 * count:3 * count]
    in_sem, out_sem = refs[3 * count:]
    loads = [
        pltpu.make_async_copy(sources[k], held[k], in_sem.at[k]) for k in range(count)
    ]
    stores = [
        pltpu.make_async_copy(held[k], targets[k], out_sem.at[k]) for k in range(count)
    ]
    for load in loads:
        load.start()
    for load, store in zip(loads, stores):
        load.wait()
        store.start()
    for store in stores:
        store.wait()


def store_all(arrays):
    count = len(arrays)
    return pl.pallas_call(
        functools.partial(store_kernel, count),
        out_shape=tuple(jax.ShapeDtypeStruct(a.shape, a.dtype) for a in arrays),
        in_specs=[pl.BlockSpec(memory_space=pl.ANY)] * count,
        out_specs=(pl.BlockSpec(memory_space=pl.ANY),) * count,
        scratch_shapes=[pltpu.VMEM(a.shape, a.dtype) for a in arrays]
        + [pltpu.SemaphoreType.DMA((count,)), pltpu.SemaphoreType.DMA((count,))],
        name="store_results",
    )(*arrays)


def shards(
    n, resp_query, resp_key, resp_value, direction, ratio, lengths, partner, prompt_key, prompt_value
):
    rows = resp_query.shape[2]
    half, key_width = prompt_key.shape
    kv_local = key_width // HEAD_DIM
    lanes = rows * resp_query.shape[3] // key_width
    keys = 2 * half + rows
    block = min(BLOCK, half)
    blocks = half // block
    unit = min(UNIT, block)
    count = kv_local * (half // unit)
    vmem = pl.BlockSpec(memory_space=pltpu.VMEM)
    smem = pl.BlockSpec(memory_space=pltpu.SMEM)
    dma = pltpu.SemaphoreType.DMA
    results = pl.pallas_call(
        functools.partial(kernel, n),
        out_shape=(
            jax.ShapeDtypeStruct(resp_query.shape, BF16),
            jax.ShapeDtypeStruct(resp_key.shape, BF16),
            jax.ShapeDtypeStruct(resp_value.shape, BF16),
            jax.ShapeDtypeStruct(prompt_key.shape, BF16),
            jax.ShapeDtypeStruct(prompt_value.shape, BF16),
        ),
        in_specs=[smem, smem] + [vmem] * 7,
        out_specs=(vmem,) * 5,
        scratch_shapes=[
            pltpu.VMEM((2 * n, 1, HEAD_DIM), F32),
            pltpu.VMEM((kv_local, lanes, HEAD_DIM), BF16),
            pltpu.VMEM((kv_local, lanes, HEAD_DIM), BF16),
            pltpu.VMEM((kv_local, half, HEAD_DIM), BF16),
            pltpu.VMEM((kv_local, half, HEAD_DIM), BF16),
            pltpu.VMEM((kv_local, keys, lanes), F32),
            pltpu.VMEM((kv_local, keys, lanes), F32),
            pltpu.VMEM((kv_local, keys, lanes), BF16),
            pltpu.VMEM((count, unit, 2 * HEAD_DIM), BF16),
            pltpu.VMEM((count, unit, 2 * HEAD_DIM), BF16),
            pltpu.VMEM((kv_local, half, 2 * HEAD_DIM), F32),
            pltpu.VMEM((2 * count, unit, 2 * HEAD_DIM), BF16),
            pltpu.VMEM((2 * count, unit, 2 * HEAD_DIM), BF16),
            dma((2 * n - 1,)), dma((2 * n - 1,)),
            dma((2 * kv_local,)), dma((2 * kv_local,)),
            dma((count,)), dma((count,)),
            dma((2 * count,)), dma((2 * count,)),
        ],
        compiler_params=pltpu.CompilerParams(
            collective_id=0, has_side_effects=True, vmem_limit_bytes=60 * 1024 * 1024
        ),
        name="shared_prompt_backward",
    )(lengths, partner, ratio, resp_query, resp_key, resp_value, direction, prompt_key, prompt_value)
    return store_all(results)


def solution(mesh):
    per_response = P("pair", "seq", None, "head")
    per_prompt = P("pair", "head")
    in_specs = (
        per_response, per_response, per_response, per_response,
        P("pair", "seq", None), P("pair", "seq"), P(), per_prompt, per_prompt,
    )
    out_specs = (per_response, per_response, per_response, per_prompt, per_prompt)
    return jax.shard_map(
        functools.partial(shards, mesh.shape["seq"]),
        mesh=mesh, in_specs=in_specs, out_specs=out_specs, check_vma=False,
    )
```

profile of v0, /device:TPU:0, one launch (start us, length us, event | category | flops | bytes accessed | tf_op | source)
XLA Modules:
  0.0 52.0 jit_solution(9062010866715320942)
XLA Ops:
  1.3 48.5 %shared_prompt_backward.1 = (bf16[1,1,256,1024]{3,2,1,0:T(8,128)(2,1)}, bf16[1,1,256,256]{3,2,1,0:T(8,128)(2,1)}, bf16[1,1,256,256]{3,2,1,0:T(8,128)(2,1)}, bf16[512,256]{1,0:T(8,128)(2,1)}, bf16[512,256]{1,0:T(8,128)(2,1)}) custom-call(s32[1,1]{1,0:T(1,128)S(6)} %copy.14.lengths, s32[4]{0:T(128)} %partner.1, f32[1,1,256]{2,1,0:T(1,128)} %ratio.1, ...), custom_call_target="tpu_custom_call" | custom-call | tf_op jit(solution)/shard_map/shared_prompt_backward/pallas_call | solution.py:361
  49.8 2.2 %store_results.1 = (bf16[1,1,256,1024]{3,2,1,0:T(8,128)(2,1)}, bf16[1,1,256,256]{3,2,1,0:T(8,128)(2,1)}, bf16[1,1,256,256]{3,2,1,0:T(8,128)(2,1)}, bf16[512,256]{1,0:T(8,128)(2,1)}, bf16[512,256]{1,0:T(8,128)(2,1)}) custom-call(bf16[1,1,256,1024]{3,2,1,0:T(8,128)(2,1)} %get-tuple-element.10.refs_0_, bf16[1,1,256,256]{3,2,1,0:T(8,128)(2,1)} %get-tuple-element.11.refs_1_, ...), custom_call_target="tpu_custom_call" | custom-call | tf_op jit(solution)/shard_map/store_results/pallas_call | solution.py:335
where the time goes:
time: 52.2 us; the launch traced here: 52 us
  Pallas kernels  50.7 us (97%)
  between operations  1.29 us (2%)
    pallas_call x1, Pallas kernels, shards(): pl.pallas_call(functools.partial(kernel, n), out_shape=(jax.ShapeDtypeStr...  48.5 us
    pallas_call x1, Pallas kernels, store_all(): pl.pallas_call(functools.partial(store_kernel, count), out_shape=tuple((j...  2.18 us

commit v1 on v0

v1 whole, which is shorter than its diff:
```python
import functools
import math

import jax
import jax.numpy as jnp
from jax import lax
from jax.experimental import pallas as pl
from jax.experimental.pallas import tpu as pltpu
from jax.sharding import PartitionSpec as P

HEAD_DIM = 128
DPO_BETA = 0.1
UNIT = 128
SLAB = 8
LAGS = (4, 8, 12)
PER_SLOT = 2
MESH = pl.DeviceIdType.MESH
NT = (((1,), (1,)), ((), ()))
TN = (((0,), (0,)), ((), ()))
F32 = jnp.float32
BF16 = jnp.bfloat16


def dot_nt(a, b):
    return lax.dot_general(a, b, NT, preferred_element_type=F32)


def dot_tn(a, b):
    return lax.dot_general(a, b, TN, preferred_element_type=F32)


def sizes(n, half):
    paired = n % 2 == 0
    part = half // 2
    return paired, part, part // 2, min(UNIT, part)


def kernel(
    n, lengths_in, partner_in, ratio_in, q_in, rk_in, rv_in, dir_in, pk_in, pv_in,
    qg_out, rkg_out, rvg_out, pkg_out, pvg_out,
    lengths, partner, ratio, table, held, pk_far, pv_far,
    s_buf, dp_buf, ds_buf, x_send, x_recv, acc, c_send, c_recv,
    small_sem, load_sem, tab_send_sem, tab_recv_sem, pair_sem,
    near_send_sem, near_recv_sem, relay_send_sem, relay_recv_sem,
    x_send_sem, x_recv_sem, c_send_sem, c_recv_sem,
):
    ns = jax.named_scope
    rows = q_in.shape[2]
    half = pk_in.shape[0]
    kv_local = rk_in.shape[3] // HEAD_DIM
    group = q_in.shape[3] // rk_in.shape[3]
    lanes = rows * group
    paired, part, chunk, unit = sizes(n, half)
    units = half // unit
    per_part = part // unit
    count = 2 * kv_local * units
    scale = 1.0 / math.sqrt(HEAD_DIM)
    exp_scale = scale * math.log2(math.e)
    side = lax.axis_index("pair")
    seq = lax.axis_index("seq")
    head = lax.axis_index("head")
    flat = side * n + seq
    parity = lax.rem(seq, 2)
    pair_dev = (1 - side, seq, head)

    def seq_dev(way):
        return (side, lax.rem(seq + way + n, n), head)

    def exists(way):
        return (seq + way >= 0) & (seq + way < n)

    barrier = pltpu.get_barrier_semaphore()
    pl.semaphore_signal(barrier, inc=1, device_id=pair_dev, device_id_type=MESH)
    for way in (1, -1):
        @pl.when(exists(way))
        def _():
            pl.semaphore_signal(barrier, inc=1, device_id=seq_dev(way), device_id_type=MESH)

    def cols_of(k):
        return slice(k * HEAD_DIM, (k + 1) * HEAD_DIM)

    small = [
        pltpu.make_async_copy(ratio_in, ratio, small_sem.at[0]),
        pltpu.make_async_copy(lengths_in, lengths, small_sem.at[1]),
        pltpu.make_async_copy(partner_in, partner, small_sem.at[2]),
    ]
    at_q = half
    at_rk = at_q + lanes
    at_g = at_rk + rows
    at_pv = at_g + lanes
    at_rv = at_pv + half
    groups = ((0, at_q), (at_q, at_g), (at_g, at_rv + rows))
    small[0].start()
    small[1].start()
    for i in range(kv_local):
        loads = [(pk_in.at[:, cols_of(i)], 0, half, 0)]
        for g in range(group):
            loads.append((q_in.at[0, 0, :, cols_of(i * group + g)], at_q + g * rows, rows, 1))
        loads.append((rk_in.at[0, 0, :, cols_of(i)], at_rk, rows, 1))
        loads.append((pv_in.at[:, cols_of(i)], at_pv, half, 2))
        for g in range(group):
            loads.append((dir_in.at[0, 0, :, cols_of(i * group + g)], at_g + g * rows, rows, 2))
        loads.append((rv_in.at[0, 0, :, cols_of(i)], at_rv, rows, 2))
        for src, at, size, which in loads:
            pltpu.make_async_copy(src, held.at[i, at:at + size, :], load_sem.at[3 * i + which]).start()
    small[2].start()

    def loaded(i, which):
        with ns("loads"):
            whole = held.at[i, groups[which][0]:groups[which][1], :]
            pltpu.make_async_copy(whole, whole, load_sem.at[3 * i + which]).wait()

    def queries(i):
        return held[i, at_q:at_q + lanes, :]

    def grads(i):
        return held[i, at_g:at_g + lanes, :]

    def near_rows(i, at, name):
        at, size = (at[1], rows) if name == "resp" else (at[0] + name * part, part)
        return held[i, at:at + size, :]

    direct, relayed = {}, {}
    for i in range(kv_local):
        for which, (at, dst) in enumerate(((0, pk_far), (at_pv, pv_far))):
            slot = 2 * i + which
            if paired and slot > 0:
                size, first = chunk, parity * part
            else:
                size, first = half, 0
            direct[slot], relayed[slot] = [], []
            for c in range(2 if size == chunk else 1):
                row = pl.multiple_of(first + c * size, size)
                span = pl.ds(row, size)
                direct[slot].append(pltpu.make_async_remote_copy(
                    src_ref=held.at[i, pl.ds(pl.multiple_of(at + row, chunk), size), :], dst_ref=dst.at[i, span, :],
                    send_sem=near_send_sem.at[slot], recv_sem=near_recv_sem.at[2 * slot + c],
                    device_id=pair_dev, device_id_type=MESH))
                if size == chunk:
                    relayed[slot].append(pltpu.make_async_remote_copy(
                        src_ref=dst.at[i, span, :], dst_ref=dst.at[i, span, :],
                        send_sem=relay_send_sem.at[slot], recv_sem=relay_recv_sem.at[slot],
                        device_id=(side, lax.rem(seq + 1 - 2 * parity + n, n), head),
                        device_id_type=MESH))

    def whole_of(slot, send_sem, recv_sem, first):
        i, which = slot // 2, slot % 2
        span = pl.ds(pl.multiple_of(first * part, part), part)
        ref = (pk_far, pv_far)[which].at[i, span, :]
        return pltpu.make_async_remote_copy(
            src_ref=ref, dst_ref=ref, send_sem=send_sem.at[slot], recv_sem=recv_sem.at[slot],
            device_id=pair_dev, device_id_type=MESH)

    def give(slot):
        for copy in direct[slot]:
            copy.start()

    def relay(slot, c):
        with ns("relay"):
            direct[slot][c].wait_recv()
            if relayed[slot]:
                relayed[slot][c].start()

    def relay_all(slot):
        for c in range(len(direct[slot])):
            relay(slot, c)

    def wait_far(slot):
        if relayed[slot]:
            with ns("wait2"):
                whole_of(slot, relay_send_sem, relay_recv_sem, 1 - parity).wait_recv()

    def sent_far(slot):
        if relayed[slot]:
            whole_of(slot, near_send_sem, relay_recv_sem, parity).wait_send()
            whole_of(slot, relay_send_sem, relay_recv_sem, parity).wait_send()
        else:
            direct[slot][0].wait_send()

    tab_pair = pltpu.make_async_remote_copy(
        src_ref=table.at[seq, side], dst_ref=table.at[seq, side],
        send_sem=pair_sem.at[0], recv_sem=pair_sem.at[1],
        device_id=pair_dev, device_id_type=MESH)

    def tab_copy(k, way):
        turn = (1 - way) // 2
        return pltpu.make_async_remote_copy(
            src_ref=table.at[seq - way * k], dst_ref=table.at[seq - way * k],
            send_sem=tab_send_sem.at[turn], recv_sem=tab_recv_sem.at[2 * k + turn],
            device_id=seq_dev(way), device_id_type=MESH)

    def came_from(k, way):
        return (seq - way * k >= 0) & (seq - way * k < n)

    def tab_step(k):
        if k == 0:
            tab_pair.wait_recv()
        for way in (1, -1):
            if k > 0:
                @pl.when(came_from(k, way))
                def _():
                    tab_copy(k - 1, way).wait_recv()

                @pl.when(came_from(k - 1, way) & exists(way))
                def _():
                    tab_copy(k - 1, way).wait_send()
            if k < n - 1:
                @pl.when(came_from(k, way) & exists(way))
                def _():
                    tab_copy(k, way).start()

    steps = list(range(n))
    per_call = -(-(n - 1) // 3)

    def tab_some(all_left=False):
        with ns("tab"):
            for _ in range(n if all_left else per_call if steps and steps[0] else 1):
                if steps:
                    tab_step(steps.pop(0))

    def weights():
        zero = jnp.zeros((1, HEAD_DIM), F32)
        mine = partner[seq]
        rejected, chosen = zero, zero
        for r in range(n):
            rejected = rejected + jnp.where(mine == r, table[r, 1], 0.0)
            chosen = chosen + jnp.where(partner[r] == seq, table[r, 0], 0.0)
        pulled_c = 1.0 / (1.0 + jnp.exp(DPO_BETA * (table[seq, 0] - rejected)))
        pulled_r = 1.0 / (1.0 + jnp.exp(DPO_BETA * (chosen - table[seq, 1])))
        own = jnp.where(side == 0, -pulled_c, pulled_r)
        other = jnp.where(side == 0, pulled_r, -pulled_c)
        return own, other

    far_at, own_at, resp_at = 0, half, 2 * half

    def score(i, at, keys, masked=False):
        scores = dot_nt(keys, queries(i))
        if masked:
            key_pos = lax.broadcasted_iota(jnp.int32, scores.shape, 0)
            row_pos = lax.rem(lax.broadcasted_iota(jnp.int32, scores.shape, 1), rows)
            scores = jnp.where((key_pos <= row_pos) & (key_pos < length), scores, -jnp.inf)
        size = scores.shape[0]
        s_buf[i, at:at + size, :] = scores
        top = jnp.max(scores, axis=0, keepdims=True)
        shift = top * exp_scale
        total = jnp.zeros((SLAB, lanes), F32)
        for r in range(0, size, SLAB):
            span = slice(at + r, at + r + SLAB)
            e = jnp.exp2(s_buf[i, span, :] * exp_scale - shift)
            s_buf[i, span, :] = e
            total = total + e
        return top, jnp.sum(total, axis=0, keepdims=True)

    def prob_grad(i, at, values):
        dp = dot_nt(values, grads(i))
        size = dp.shape[0]
        dp_buf[i, at:at + size, :] = dp
        total = jnp.zeros((SLAB, lanes), F32)
        for r in range(0, size, SLAB):
            span = slice(at + r, at + r + SLAB)
            total = total + s_buf[i, span, :] * dp[r:r + SLAB]
        return jnp.sum(total, axis=0, keepdims=True)

    def value_grad(i, at, size, share):
        prob = (s_buf[i, at:at + size, :] * share).astype(BF16)
        return jnp.dot(prob, grads(i), preferred_element_type=F32)

    def key_grad(i, at, size, share, delta):
        ds = (s_buf[i, at:at + size, :] * share * (dp_buf[i, at:at + size, :] - delta)).astype(BF16)
        ds_buf[i, at:at + size, :] = ds
        return jnp.dot(ds, queries(i), preferred_element_type=F32)

    def unit_of(i, kind, r):
        return (2 * i + kind) * units + r

    def x_copy(u):
        return pltpu.make_async_remote_copy(
            src_ref=x_send.at[u], dst_ref=x_recv.at[u],
            send_sem=x_send_sem.at[0], recv_sem=x_recv_sem.at[u],
            device_id=pair_dev, device_id_type=MESH)

    def send_far(i, kind, b, grads):
        for k in range(per_part):
            u = unit_of(i, kind, b * per_part + k)
            x_send[u] = grads[k * unit:(k + 1) * unit].astype(BF16)
            x_copy(u).start()

    def keep_own(i, kind, b, grads):
        for k in range(per_part):
            acc[unit_of(i, kind, b * per_part + k)] = grads[k * unit:(k + 1) * unit]

    first_way = jnp.where(2 * seq < n, 1, -1)

    def chain_copy(u, way):
        turn = (1 - way) // 2
        return pltpu.make_async_remote_copy(
            src_ref=c_send.at[turn, u], dst_ref=c_recv.at[turn, u],
            send_sem=c_send_sem.at[turn], recv_sem=c_recv_sem.at[2 * u + turn],
            device_id=seq_dev(way), device_id_type=MESH)

    def chain_pass(u, way):
        turn = (1 - way) // 2
        chain_copy(u, way).wait_recv()
        c_send[turn, u] = (acc[u] + c_recv[turn, u].astype(F32)).astype(BF16)
        chain_copy(u, way).start()

    def chain_enter(u, own, other):
        factor = scale if (u // units) % 2 else 1.0
        with ns("xwait"):
            x_copy(u).wait_recv()
        acc[u] = acc[u] * (own * factor) + x_recv[u].astype(F32) * (other * factor)

        @pl.when(exists(first_way) & jnp.logical_not(exists(-first_way)))
        def _():
            c_send[(1 - first_way) // 2, u] = acc[u].astype(BF16)
            chain_copy(u, first_way).start()

    def chain_inward(u):
        @pl.when(exists(first_way) & exists(-first_way))
        def _():
            with ns("inward"):
                chain_pass(u, first_way)

    def chain_outward(u):
        @pl.when(exists(first_way) & exists(-first_way))
        def _():
            with ns("outward"):
                chain_pass(u, -first_way)
            write(u)

    def chain_end(u):
        @pl.when(jnp.logical_not(exists(-first_way)))
        def _():
            @pl.when(exists(first_way))
            def _():
                with ns("endwait"):
                    chain_copy(u, -first_way).wait_recv()
            write(u)

    def write(u):
        for way in (1, -1):
            @pl.when(exists(-way))
            def _():
                acc[u] += c_recv[(1 - way) // 2, u].astype(F32)
        i, kind, r = u // (2 * units), u // units % 2, u % units
        out = pkg_out if kind else pvg_out
        out[r * unit:(r + 1) * unit, cols_of(i)] = acc[u].astype(BF16)

    def slot(s, own, other):
        for lag, step in zip(LAGS[::-1], (chain_end, chain_outward, chain_inward)):
            if 0 <= s - lag < count:
                step(s - lag)
        if s < count:
            chain_enter(s, own, other)

    def query(i, own):
        total = jnp.zeros((HEAD_DIM, lanes), F32)
        for at, keys in (
            (own_at, held[i, :half, :]), (resp_at, held[i, at_rk:at_rk + rows, :]), (far_at, pk_far[i])
        ):
            total = total + dot_tn(keys, ds_buf[i, at:at + keys.shape[0], :])
        factor = own * scale
        for g in range(group):
            qg_out[0, 0, :, cols_of(i * group + g)] = (
                total[:, g * rows:(g + 1) * rows].T * factor).astype(BF16)

    def resp(i, own):
        rvg_out[0, 0, :, cols_of(i)] = (
            value_grad(i, resp_at, rows, share[i, "resp"]) * own).astype(BF16)
        rkg_out[0, 0, :, cols_of(i)] = (
            key_grad(i, resp_at, rows, share[i, "resp"], delta[i]) * (own * scale)).astype(BF16)

    tops, totals, deltas, share, delta = {}, {}, {}, {}, {}

    def at_of(name):
        return resp_at if name == "resp" else own_at + name * part

    def near(i, name):
        with ns(f"near{i}{name}"):
            tops[i, name], totals[i, name] = score(
                i, at_of(name), near_rows(i, (0, at_rk), name), name == "resp")

    def near_delta(i, name):
        with ns(f"dnear{i}{name}"):
            deltas[i, name] = prob_grad(i, at_of(name), near_rows(i, (at_pv, at_rv), name))

    def far(i, b):
        with ns(f"far{i}{b}"):
            at = far_at + b * part
            tops[i, f"far{b}"], totals[i, f"far{b}"] = score(i, at, pk_far[i, b * part:(b + 1) * part, :])

    def far_delta(i, b):
        with ns(f"dfar{i}{b}"):
            at = far_at + b * part
            deltas[i, f"far{b}"] = prob_grad(i, at, pv_far[i, b * part:(b + 1) * part, :])

    names = ("far0", "far1", 0, 1, "resp")

    def stats(i):
        top = functools.reduce(jnp.maximum, [tops[i, name] for name in names])
        part_of = {name: jnp.exp2((tops[i, name] - top) * exp_scale) for name in names}
        total = sum(totals[i, name] * part_of[name] for name in names)
        row = lax.rem(lax.broadcasted_iota(jnp.int32, (1, lanes), 1), rows)
        inv = jnp.where(row < length, 1.0 / total, 0.0)
        for name in names:
            share[i, name] = part_of[name] * inv

    def far_values(i, b):
        with ns(f"vfar{i}{b}"):
            send_far(i, 0, b, value_grad(i, far_at + b * part, part, share[i, f"far{b}"]))

    def far_keys(i, b):
        with ns(f"kfar{i}{b}"):
            send_far(i, 1, b, key_grad(i, far_at + b * part, part, share[i, f"far{b}"], delta[i]))

    def own_values(i, b):
        with ns(f"vown{i}{b}"):
            keep_own(i, 0, b, value_grad(i, own_at + b * part, part, share[i, b]))

    def own_keys(i, b):
        with ns(f"kown{i}{b}"):
            keep_own(i, 1, b, key_grad(i, own_at + b * part, part, share[i, b], delta[i]))

    def sum_delta(i):
        delta[i] = sum(deltas[i, name] * share[i, name] for name in names)

    with ns("small"):
        small[0].wait()
        small[1].wait()
    length = lengths[0, 0]
    position = lax.broadcasted_iota(jnp.int32, (1, rows), 1)
    own_sum = jnp.sum(jnp.where(position < length, ratio[0], 0.0), axis=1, keepdims=True)
    table[seq, side] = jnp.broadcast_to(own_sum, (1, HEAD_DIM))
    with ns("barrier"):
        pl.semaphore_wait(barrier, 1 + jnp.where(exists(1), 1, 0) + jnp.where(exists(-1), 1, 0))
    tab_pair.start()
    loaded(0, 0)
    give(0)
    last = kv_local - 1
    loaded(0, 1)
    near(0, 0)
    loaded(0, 2)
    give(1)
    for i in range(1, kv_local):
        for which in range(3):
            loaded(i, which)
        give(2 * i)
        give(2 * i + 1)
    near(0, 1)
    near(0, "resp")
    tab_some()
    if last:
        near(last, 0)
        near(last, 1)
        near(last, "resp")
    near_delta(0, 0)
    near_delta(0, 1)
    tab_some()
    near_delta(0, "resp")
    relay_all(0)
    far(0, 0)
    relay(1, 0)
    far(0, 1)
    stats(0)
    if len(direct[1]) > 1:
        relay(1, 1)
    far_values(0, 0)
    far_values(0, 1)
    tab_some()
    if last:
        relay_all(2 * last)
    own_values(0, 0)
    own_values(0, 1)
    wait_far(1)
    far_delta(0, 0)
    far_delta(0, 1)
    sum_delta(0)
    far_keys(0, 0)
    far_keys(0, 1)
    tab_some(True)
    with ns("small"):
        small[2].wait()
    own, other = weights()

    def resp_work(i):
        with ns(f"resp{i}"):
            resp(i, own)

    def query_work(i):
        with ns(f"query{i}"):
            query(i, own)

    work = [lambda: own_keys(0, 0), lambda: own_keys(0, 1)]
    if last:
        work += [
            lambda: relay_all(2 * last + 1),
            lambda: near_delta(last, 0), lambda: near_delta(last, 1), lambda: near_delta(last, "resp"),
            lambda: (wait_far(2 * last), far(last, 0)), lambda: (far(last, 1), stats(last)),
            lambda: far_values(last, 0), lambda: far_values(last, 1),
            lambda: (wait_far(2 * last + 1), far_delta(last, 0)),
            lambda: (far_delta(last, 1), sum_delta(last)),
            lambda: far_keys(last, 0), lambda: far_keys(last, 1),
            lambda: own_values(last, 0), lambda: own_values(last, 1),
            lambda: own_keys(last, 0), lambda: own_keys(last, 1),
        ]
    work += [lambda i=i: resp_work(i) for i in range(kv_local)]
    work += [lambda i=i: query_work(i) for i in range(kv_local)]
    for s in range(count + LAGS[-1]):
        slot(s, own, other)
        for _ in range(PER_SLOT):
            if work:
                work.pop(0)()
    while work:
        work.pop(0)()

    with ns("sendwait"):
        tab_pair.wait_send()
        for slot_ in range(2 * kv_local):
            sent_far(slot_)
        pltpu.make_async_remote_copy(
            src_ref=x_send, dst_ref=x_recv, send_sem=x_send_sem.at[0], recv_sem=x_recv_sem.at[0],
            device_id=pair_dev, device_id_type=MESH).wait_send()
        for way in (1, -1):
            @pl.when(exists(way))
            def _():
                turn = (1 - way) // 2
                pltpu.make_async_remote_copy(
                    src_ref=c_send.at[turn], dst_ref=c_recv.at[turn],
                    send_sem=c_send_sem.at[turn], recv_sem=c_recv_sem.at[0],
                    device_id=seq_dev(way), device_id_type=MESH).wait_send()


def store_kernel(count, *refs):
    sources, targets, sem = refs[:count], refs[count:2 * count], refs[2 * count]
    stores = [pltpu.make_async_copy(sources[k], targets[k], sem.at[k]) for k in range(count)]
    for store in stores:
        store.start()
    for store in stores:
        store.wait()


def store_all(arrays):
    count = len(arrays)
    return pl.pallas_call(
        functools.partial(store_kernel, count),
        out_shape=tuple(jax.ShapeDtypeStruct(a.shape, a.dtype) for a in arrays),
        in_specs=[pl.BlockSpec(memory_space=pltpu.VMEM)] * count,
        out_specs=(pl.BlockSpec(memory_space=pl.ANY),) * count,
        scratch_shapes=[pltpu.SemaphoreType.DMA((count,))],
        compiler_params=pltpu.CompilerParams(vmem_limit_bytes=1024 * 1024),
        name="store_results",
    )(*arrays)


def shards(
    n, resp_query, resp_key, resp_value, direction, ratio, lengths, partner, prompt_key, prompt_value
):
    rows = resp_query.shape[2]
    half, key_width = prompt_key.shape
    kv_local = key_width // HEAD_DIM
    heads = resp_query.shape[3] // HEAD_DIM
    lanes = rows * heads // kv_local
    keys = 2 * half + rows
    unit = sizes(n, half)[-1]
    count = 2 * kv_local * (half // unit)
    hbm = pl.BlockSpec(memory_space=pltpu.HBM)
    dma = pltpu.SemaphoreType.DMA
    results = pl.pallas_call(
        functools.partial(kernel, n),
        out_shape=tuple(
            pltpu.VMEM(a.shape, BF16)
            for a in (resp_query, resp_key, resp_value, prompt_key, prompt_value)
        ),
        in_specs=[hbm] * 9,
        scratch_shapes=[
            pltpu.SMEM((1, 1), jnp.int32),
            pltpu.SMEM((n,), jnp.int32),
            pltpu.VMEM((1, 1, rows), F32),
            pltpu.VMEM((n, 2, 1, HEAD_DIM), F32),
            pltpu.VMEM((kv_local, 2 * (half + lanes + rows), HEAD_DIM), BF16),
            pltpu.VMEM((kv_local, half, HEAD_DIM), BF16),
            pltpu.VMEM((kv_local, half, HEAD_DIM), BF16),
            pltpu.VMEM((kv_local, keys, lanes), F32),
            pltpu.VMEM((kv_local, keys, lanes), F32),
            pltpu.VMEM((kv_local, keys, lanes), BF16),
            pltpu.VMEM((count, unit, HEAD_DIM), BF16),
            pltpu.VMEM((count, unit, HEAD_DIM), BF16),
            pltpu.VMEM((count, unit, HEAD_DIM), F32),
            pltpu.VMEM((2, count, unit, HEAD_DIM), BF16),
            pltpu.VMEM((2, count, unit, HEAD_DIM), BF16),
            dma((3,)), dma((3 * kv_local,)), dma((2,)), dma((2 * max(n - 1, 1),)), dma((2,)),
            dma((2 * kv_local,)), dma((4 * kv_local,)), dma((2 * kv_local,)), dma((2 * kv_local,)),
            dma((1,)), dma((count,)), dma((2,)), dma((2 * count,)),
        ],
        compiler_params=pltpu.CompilerParams(
            collective_id=0, has_side_effects=True, vmem_limit_bytes=48 * 1024 * 1024
        ),
        name="shared_prompt_backward",
    )(lengths, *(
        pltpu.with_memory_space_constraint(a, pltpu.HBM)
        for a in (partner, ratio, resp_query, resp_key, resp_value, direction, prompt_key, prompt_value)
    ))
    return store_all(results)


def solution(mesh):
    per_response = P("pair", "seq", None, "head")
    per_prompt = P("pair", "head")
    in_specs = (
        per_response, per_response, per_response, per_response,
        P("pair", "seq", None), P("pair", "seq"), P(), per_prompt, per_prompt,
    )
    out_specs = (per_response, per_response, per_response, per_prompt, per_prompt)
    return jax.shard_map(
        functools.partial(shards, mesh.shape["seq"]),
        mesh=mesh, in_specs=in_specs, out_specs=out_specs, check_vma=False,
    )
```

time: 52.2 us -> 40.9 us (0.78)
  Pallas kernels: 50.7 us -> 39.4 us
    pallas_call x1, Pallas kernels: 48.5 us -> 38.3 us  [shards(): pl.pallas_call(functools.partial(kernel, n), out_shape=tuple((pltpu.VMEM(...]
    pallas_call x1, Pallas kernels: 2.18 us -> 1.09 us  [store_all(): pl.pallas_call(functools.partial(store_kernel, count), out_shape=tuple((j...]
where the time goes in v1:
time: 40.9 us; the launch traced here: 40.7 us
  Pallas kernels  39.4 us (96%)
  between operations  1.29 us (3%)
    pallas_call x1, Pallas kernels, shards(): pl.pallas_call(functools.partial(kernel, n), out_shape=tuple((pltpu.VMEM(...  38.3 us
    pallas_call x1, Pallas kernels, store_all(): pl.pallas_call(functools.partial(store_kernel, count), out_shape=tuple((j...  1.09 us

profile of v1, /device:TPU:0, one launch (start us, length us, event | category | flops | bytes accessed | tf_op | source)
XLA Modules:
  0.0 40.7 jit_solution(8845136662629597566)
XLA Ops:
  1.3 38.3 %shared_prompt_backward.1 = (bf16[1,1,256,1024]{3,2,1,0:T(8,128)(2,1)S(1)}, bf16[1,1,256,256]{3,2,1,0:T(8,128)(2,1)S(1)}, bf16[1,1,256,256]{3,2,1,0:T(8,128)(2,1...) custom-call(s32[1,1]{1,0:T(1,128)S(6)} %copy.14.lengths_in, s32[4]{0:T(128)} %partner_in.1, ...), custom_call_target="tpu_custom_call" | custom-call | tf_op jit(solution)/shard_map/shared_prompt_backward/pallas_call | solution.py:568
  39.6 1.1 %store_results.1 = (bf16[1,1,256,1024]{3,2,1,0:T(8,128)(2,1)}, bf16[1,1,256,256]{3,2,1,0:T(8,128)(2,1)}, bf16[1,1,256,256]{3,2,1,0:T(8,128)(2,1)}, bf16[512,256]{1,0:T(8,128)(2,1)}, bf16[512,256]{1,0:T(8,128)(2,1)}) custom-call(bf16[1,1,256,1024]{3,2,1,0:T(8,128)(2,1)S(1)} %get-tuple-element.10.refs_0_, ...), custom_call_target="tpu_custom_call" | custom-call | tf_op jit(solution)/shard_map/store_results/pallas_call | solution.py:544

commit v2 on v1

--- a/solution.py
+++ b/solution.py
@@ -12,8 +12,7 @@
 DPO_BETA = 0.1
 UNIT = 128
 SLAB = 8
-LAGS = (4, 8, 12)
-PER_SLOT = 2
+RATE, HOP, LEAD = 0.7, 3.5, 0.6
 MESH = pl.DeviceIdType.MESH
 NT = (((1,), (1,)), ((), ()))
 TN = (((0,), (0,)), ((), ()))
@@ -124,19 +123,17 @@
     for i in range(kv_local):
         for which, (at, dst) in enumerate(((0, pk_far), (at_pv, pv_far))):
             slot = 2 * i + which
-            if paired and slot > 0:
-                size, first = chunk, parity * part
-            else:
-                size, first = half, 0
+            shared = paired and slot > 0
+            size, first = (chunk, parity * part) if shared else (part, 0)
             direct[slot], relayed[slot] = [], []
-            for c in range(2 if size == chunk else 1):
+            for c in range(2):
                 row = pl.multiple_of(first + c * size, size)
                 span = pl.ds(row, size)
                 direct[slot].append(pltpu.make_async_remote_copy(
                     src_ref=held.at[i, pl.ds(pl.multiple_of(at + row, chunk), size), :], dst_ref=dst.at[i, span, :],
                     send_sem=near_send_sem.at[slot], recv_sem=near_recv_sem.at[2 * slot + c],
                     device_id=pair_dev, device_id_type=MESH))
-                if size == chunk:
+                if shared:
                     relayed[slot].append(pltpu.make_async_remote_copy(
                         src_ref=dst.at[i, span, :], dst_ref=dst.at[i, span, :],
                         send_sem=relay_send_sem.at[slot], recv_sem=relay_recv_sem.at[slot],
@@ -175,7 +172,10 @@
             whole_of(slot, near_send_sem, relay_recv_sem, parity).wait_send()
             whole_of(slot, relay_send_sem, relay_recv_sem, parity).wait_send()
         else:
-            direct[slot][0].wait_send()
+            i, ref = slot // 2, (pk_far, pv_far)[slot % 2]
+            pltpu.make_async_remote_copy(
+                src_ref=ref.at[i], dst_ref=ref.at[i], send_sem=near_send_sem.at[slot],
+                recv_sem=relay_recv_sem.at[slot], device_id=pair_dev, device_id_type=MESH).wait_send()
 
     tab_pair = pltpu.make_async_remote_copy(
         src_ref=table.at[seq, side], dst_ref=table.at[seq, side],
@@ -346,13 +346,6 @@
         out = pkg_out if kind else pvg_out
         out[r * unit:(r + 1) * unit, cols_of(i)] = acc[u].astype(BF16)
 
-    def slot(s, own, other):
-        for lag, step in zip(LAGS[::-1], (chain_end, chain_outward, chain_inward)):
-            if 0 <= s - lag < count:
-                step(s - lag)
-        if s < count:
-            chain_enter(s, own, other)
-
     def query(i, own):
         total = jnp.zeros((HEAD_DIM, lanes), F32)
         for at, keys in (
@@ -365,12 +358,15 @@
                 total[:, g * rows:(g + 1) * rows].T * factor).astype(BF16)
 
     def resp(i, own):
-        rvg_out[0, 0, :, cols_of(i)] = (
-            value_grad(i, resp_at, rows, share[i, "resp"]) * own).astype(BF16)
+        rvg_out[0, 0, :, cols_of(i)] = (held_values[i] * own).astype(BF16)
         rkg_out[0, 0, :, cols_of(i)] = (
             key_grad(i, resp_at, rows, share[i, "resp"], delta[i]) * (own * scale)).astype(BF16)
 
-    tops, totals, deltas, share, delta = {}, {}, {}, {}, {}
+    tops, totals, deltas, share, delta, held_values = {}, {}, {}, {}, {}, {}
+
+    def resp_values(i):
+        with ns(f"vresp{i}"):
+            held_values[i] = value_grad(i, resp_at, rows, share[i, "resp"])
 
     def at_of(name):
         return resp_at if name == "resp" else own_at + name * part
@@ -435,83 +431,107 @@
         pl.semaphore_wait(barrier, 1 + jnp.where(exists(1), 1, 0) + jnp.where(exists(-1), 1, 0))
     tab_pair.start()
     loaded(0, 0)
-    give(0)
+    direct[0][0].start()
     last = kv_local - 1
     loaded(0, 1)
     near(0, 0)
+    near(0, 1)
+    direct[0][1].start()
+    near(0, "resp")
     loaded(0, 2)
-    give(1)
-    for i in range(1, kv_local):
+    if last:
         for which in range(3):
-            loaded(i, which)
-        give(2 * i)
-        give(2 * i + 1)
-    near(0, 1)
-    near(0, "resp")
-    tab_some()
-    if last:
+            loaded(last, which)
         near(last, 0)
         near(last, 1)
+    give(1)
+    if last:
         near(last, "resp")
+    tab_some()
     near_delta(0, 0)
     near_delta(0, 1)
-    tab_some()
     near_delta(0, "resp")
-    relay_all(0)
+    if last:
+        give(2 * last)
+    relay(0, 0)
     far(0, 0)
-    relay(1, 0)
+    relay(0, 1)
     far(0, 1)
     stats(0)
-    if len(direct[1]) > 1:
-        relay(1, 1)
+    if last:
+        give(2 * last + 1)
+    tab_some()
     far_values(0, 0)
     far_values(0, 1)
-    tab_some()
-    if last:
-        relay_all(2 * last)
+    relay_all(1)
     own_values(0, 0)
     own_values(0, 1)
-    wait_far(1)
-    far_delta(0, 0)
-    far_delta(0, 1)
-    sum_delta(0)
-    far_keys(0, 0)
-    far_keys(0, 1)
-    tab_some(True)
-    with ns("small"):
-        small[2].wait()
-    own, other = weights()
+    if last:
+        near_delta(last, 0)
+        near_delta(last, 1)
+    tab_some()
+    if last:
+        relay_all(2 * last)
+        near_delta(last, "resp")
+    resp_values(0)
+    if last:
+        relay_all(2 * last + 1)
+
+    weight = []
+
+    def start_chain():
+        tab_some(True)
+        with ns("small"):
+            small[2].wait()
+        weight.extend(weights())
 
     def resp_work(i):
         with ns(f"resp{i}"):
-            resp(i, own)
+            resp(i, weight[0])
 
     def query_work(i):
         with ns(f"query{i}"):
-            query(i, own)
-
-    work = [lambda: own_keys(0, 0), lambda: own_keys(0, 1)]
+            query(i, weight[0])
+
+    work = [
+        (0.3, lambda: (wait_far(1), far_delta(0, 0))), (0.3, lambda: (far_delta(0, 1), sum_delta(0))),
+        (0.3, lambda: far_keys(0, 0)), (0.3, lambda: far_keys(0, 1)),
+    ]
+    work += [(0.3, lambda: own_keys(0, 0)), (0.3, lambda: own_keys(0, 1))]
     if last:
         work += [
-            lambda: relay_all(2 * last + 1),
-            lambda: near_delta(last, 0), lambda: near_delta(last, 1), lambda: near_delta(last, "resp"),
-            lambda: (wait_far(2 * last), far(last, 0)), lambda: (far(last, 1), stats(last)),
-            lambda: far_values(last, 0), lambda: far_values(last, 1),
-            lambda: (wait_far(2 * last + 1), far_delta(last, 0)),
-            lambda: (far_delta(last, 1), sum_delta(last)),
-            lambda: far_keys(last, 0), lambda: far_keys(last, 1),
-            lambda: own_values(last, 0), lambda: own_values(last, 1),
-            lambda: own_keys(last, 0), lambda: own_keys(last, 1),
+            (0.5, lambda: (wait_far(2 * last), far(last, 0))), (0.5, lambda: (far(last, 1), stats(last))),
+            (0.3, lambda: far_values(last, 0)), (0.3, lambda: far_values(last, 1)),
+            (0.3, lambda: (wait_far(2 * last + 1), far_delta(last, 0))),
+            (0.3, lambda: (far_delta(last, 1), sum_delta(last))),
+            (0.3, lambda: far_keys(last, 0)), (0.3, lambda: far_keys(last, 1)),
+            (0.3, lambda: own_values(last, 0)), (0.3, lambda: own_values(last, 1)),
+            (0.3, lambda: own_keys(last, 0)), (0.3, lambda: own_keys(last, 1)),
         ]
-    work += [lambda i=i: resp_work(i) for i in range(kv_local)]
-    work += [lambda i=i: query_work(i) for i in range(kv_local)]
-    for s in range(count + LAGS[-1]):
-        slot(s, own, other)
-        for _ in range(PER_SLOT):
-            if work:
-                work.pop(0)()
-    while work:
-        work.pop(0)()
+    if last:
+        work += [(0.2, lambda: resp_values(last))]
+    work += [(0.3, lambda i=i: resp_work(i)) for i in range(kv_local)]
+    work += [(0.65, lambda i=i: query_work(i)) for i in range(kv_local)]
+    chain = []
+    for u in range(count):
+        for hops, step in enumerate((chain_enter, chain_inward, chain_outward, chain_end)):
+            chain.append((LEAD + u * RATE + hops * HOP, hops, u, step))
+    chain.sort(key=lambda item: item[:3])
+    now = 0.0
+    while work or chain:
+        if chain and (not work or chain[0][0] <= now):
+            at, hops, u, step = chain.pop(0)
+            now = max(now, at) + 0.04
+            if not weight:
+                start_chain()
+            if hops == 0:
+                step(u, *weight)
+            else:
+                step(u)
+        else:
+            cost, step = work.pop(0)
+            step()
+            now += cost
 
     with ns("sendwait"):
         tab_pair.wait_send()

time: 40.9 us -> 38 us (0.929)
  Pallas kernels: 39.4 us -> 36.6 us
    pallas_call x1, Pallas kernels: 38.3 us -> 35.5 us  [shards(): pl.pallas_call(functools.partial(kernel, n), out_shape=tuple((pltpu.VMEM(...]
where the time goes in v2:
time: 38 us; the launch traced here: 37.9 us
  Pallas kernels  36.6 us (96%)
  between operations  1.29 us (3%)
    pallas_call x1, Pallas kernels, shards(): pl.pallas_call(functools.partial(kernel, n), out_shape=tuple((pltpu.VMEM(...  35.5 us
    pallas_call x1, Pallas kernels, store_all(): pl.pallas_call(functools.partial(store_kernel, count), out_shape=tuple((j...  1.09 us

profile of v2, /device:TPU:0, one launch (start us, length us, event | category | flops | bytes accessed | tf_op | source)
XLA Modules:
  0.0 37.9 jit_solution(11625615294596717352)
XLA Ops:
  1.3 35.5 %shared_prompt_backward.1 = (bf16[1,1,256,1024]{3,2,1,0:T(8,128)(2,1)S(1)}, bf16[1,1,256,256]{3,2,1,0:T(8,128)(2,1)S(1)}, bf16[1,1,256,256]{3,2,1,0:T(8,128)(2,1...) custom-call(s32[1,1]{1,0:T(1,128)S(6)} %copy.14.lengths_in, s32[4]{0:T(128)} %partner_in.1, ...), custom_call_target="tpu_custom_call" | custom-call | tf_op jit(solution)/shard_map/shared_prompt_backward/pallas_call | solution.py:588
  36.8 1.1 %store_results.1 = (bf16[1,1,256,1024]{3,2,1,0:T(8,128)(2,1)}, bf16[1,1,256,256]{3,2,1,0:T(8,128)(2,1)}, bf16[1,1,256,256]{3,2,1,0:T(8,128)(2,1)}, bf16[512,256]{1,0:T(8,128)(2,1)}, bf16[512,256]{1,0:T(8,128)(2,1)}) custom-call(bf16[1,1,256,1024]{3,2,1,0:T(8,128)(2,1)S(1)} %get-tuple-element.10.refs_0_, ...), custom_call_target="tpu_custom_call" | custom-call | tf_op jit(solution)/shard_map/store_results/pallas_call | solution.py:564

commit v3 on v2

--- a/solution.py
+++ b/solution.py
@@ -37,7 +37,7 @@
 def kernel(
     n, lengths_in, partner_in, ratio_in, q_in, rk_in, rv_in, dir_in, pk_in, pv_in,
     qg_out, rkg_out, rvg_out, pkg_out, pvg_out,
-    lengths, partner, ratio, table, held, pk_far, pv_far,
+    partner, ratio, table, held, pk_far, pv_far,
     s_buf, dp_buf, ds_buf, x_send, x_recv, acc, c_send, c_recv,
     small_sem, load_sem, tab_send_sem, tab_recv_sem, pair_sem,
     near_send_sem, near_recv_sem, relay_send_sem, relay_recv_sem,
@@ -80,8 +80,7 @@
 
     small = [
         pltpu.make_async_copy(ratio_in, ratio, small_sem.at[0]),
-        pltpu.make_async_copy(lengths_in, lengths, small_sem.at[1]),
-        pltpu.make_async_copy(partner_in, partner, small_sem.at[2]),
+        pltpu.make_async_copy(partner_in, partner, small_sem.at[1]),
     ]
     at_q = half
     at_rk = at_q + lanes
@@ -90,7 +89,6 @@
     at_rv = at_pv + half
     groups = ((0, at_q), (at_q, at_g), (at_g, at_rv + rows))
     small[0].start()
-    small[1].start()
     for i in range(kv_local):
         loads = [(pk_in.at[:, cols_of(i)], 0, half, 0)]
         for g in range(group):
@@ -102,7 +100,7 @@
         loads.append((rv_in.at[0, 0, :, cols_of(i)], at_rv, rows, 2))
         for src, at, size, which in loads:
             pltpu.make_async_copy(src, held.at[i, at:at + size, :], load_sem.at[3 * i + which]).start()
-    small[2].start()
+    small[1].start()
 
     def loaded(i, which):
         with ns("loads"):
@@ -422,8 +420,7 @@
 
     with ns("small"):
         small[0].wait()
-        small[1].wait()
-    length = lengths[0, 0]
+    length = lengths_in[0, 0]
     position = lax.broadcasted_iota(jnp.int32, (1, rows), 1)
     own_sum = jnp.sum(jnp.where(position < length, ratio[0], 0.0), axis=1, keepdims=True)
     table[seq, side] = jnp.broadcast_to(own_sum, (1, HEAD_DIM))
@@ -439,12 +436,12 @@
     direct[0][1].start()
     near(0, "resp")
     loaded(0, 2)
+    give(1)
     if last:
         for which in range(3):
             loaded(last, which)
         near(last, 0)
         near(last, 1)
-    give(1)
     if last:
         near(last, "resp")
     tab_some()
@@ -482,7 +479,7 @@
     def start_chain():
         tab_some(True)
         with ns("small"):
-            small[2].wait()
+            small[1].wait()
         weight.extend(weights())
 
     def resp_work(i):
@@ -591,9 +588,8 @@
             pltpu.VMEM(a.shape, BF16)
             for a in (resp_query, resp_key, resp_value, prompt_key, prompt_value)
         ),
-        in_specs=[hbm] * 9,
+        in_specs=[pl.BlockSpec(memory_space=pltpu.SMEM)] + [hbm] * 8,
         scratch_shapes=[
-            pltpu.SMEM((1, 1), jnp.int32),
             pltpu.SMEM((n,), jnp.int32),
             pltpu.VMEM((1, 1, rows), F32),
             pltpu.VMEM((n, 2, 1, HEAD_DIM), F32),
@@ -608,7 +604,7 @@
             pltpu.VMEM((count, unit, HEAD_DIM), F32),
             pltpu.VMEM((2, count, unit, HEAD_DIM), BF16),
             pltpu.VMEM((2, count, unit, HEAD_DIM), BF16),
-            dma((3,)), dma((3 * kv_local,)), dma((2,)), dma((2 * max(n - 1, 1),)), dma((2,)),
+            dma((2,)), dma((3 * kv_local,)), dma((2,)), dma((2 * max(n - 1, 1),)), dma((2,)),
             dma((2 * kv_local,)), dma((4 * kv_local,)), dma((2 * kv_local,)), dma((2 * kv_local,)),
             dma((1,)), dma((count,)), dma((2,)), dma((2 * count,)),
         ],

time: 38 us -> 38 us (level)
  no operation moved by 1% of the time
where the time goes in v3:
time: 38 us; the launch traced here: 37.9 us
  Pallas kernels  36.6 us (96%)
  between operations  1.29 us (3%)
    pallas_call x1, Pallas kernels, shards(): pl.pallas_call(functools.partial(kernel, n), out_shape=tuple((pltpu.VMEM(...  35.5 us
    pallas_call x1, Pallas kernels, store_all(): pl.pallas_call(functools.partial(store_kernel, count), out_shape=tuple((j...  1.09 us

profile of v3, /device:TPU:0, one launch (start us, length us, event | category | flops | bytes accessed | tf_op | source)
XLA Modules:
  0.0 37.9 jit_solution(3887304939223456534)
XLA Ops:
  1.3 35.5 %shared_prompt_backward.1 = (bf16[1,1,256,1024]{3,2,1,0:T(8,128)(2,1)S(1)}, bf16[1,1,256,256]{3,2,1,0:T(8,128)(2,1)S(1)}, bf16[1,1,256,256]{3,2,1,0:T(8,128)(2,1...) custom-call(s32[1,1]{1,0:T(1,128)S(6)} %copy.14.lengths_in, s32[4]{0:T(128)} %partner_in.1, ...), custom_call_target="tpu_custom_call" | custom-call | tf_op jit(solution)/shard_map/shared_prompt_backward/pallas_call | solution.py:585
  36.8 1.1 %store_results.1 = (bf16[1,1,256,1024]{3,2,1,0:T(8,128)(2,1)}, bf16[1,1,256,256]{3,2,1,0:T(8,128)(2,1)}, bf16[1,1,256,256]{3,2,1,0:T(8,128)(2,1)}, bf16[512,256]{1,0:T(8,128)(2,1)}, bf16[512,256]{1,0:T(8,128)(2,1)}) custom-call(bf16[1,1,256,1024]{3,2,1,0:T(8,128)(2,1)S(1)} %get-tuple-element.10.refs_0_, ...), custom_call_target="tpu_custom_call" | custom-call | tf_op jit(solution)/shard_map/store_results/pallas_call | solution.py:561
